TPU v7x, 32 devices: a whole 2x2x4 slice. The times are simulated.
32 devices in a mesh: facet: 8 (over z, y), col: 4 (over x, core).
Axes of the slice: x: 2, y: 2, z: 4, core: 2. Of those that a mesh axis runs over, the one named last changes fastest.
Arguments:
- prepared: bfloat16 [8, 2, 8192, 512], P('facet', None, None, 'col'), may hold values from -6 to 6
- sub_off: int32 [8, 4], P(None, 'col'), may hold values from 0 to 8191
- fac_off: int32 [8], replicated, may hold values from 0 to 511
- win_col: int32 [4, 128], replicated, may hold values from 0 to 255
- vis_weights: bfloat16 [8, 2, 512, 512], P('facet', None, None, 'col'), may hold values from -6 to 6
Outputs:
- facet_strips: bfloat16 [8, 2, 8192, 256], P('facet', None, 'col')
All inputs are finite; a program needn't handle non-finite values.
Results may differ from a plain program's by a relative error of at most 0.0093.
Values may be sent and summed in bfloat16 or wider, within the bound.
A program may use at most 128 MiB of HBM per device.

v0:
```python
import math
import jax
import jax.numpy as jnp
from jax import lax
from jax.sharding import PartitionSpec as P

XM = 128


def taper_curve(length):
    position = (jnp.arange(length, dtype=jnp.float32) + 0.5) / length
    return 0.3 + 0.7 * jnp.sin(math.pi * position) ** 2


def phases(row_ids, col_ids, length, sign_factor, scaling):
    products = row_ids[:, None] * col_ids[None, :] % length
    angles = 2.0 * math.pi / length * products.astype(jnp.float32)
    return (jnp.cos(angles) * scaling, sign_factor * jnp.sin(angles) * scaling)


def complex_block(real_part, imag_part):
    upper_rows = jnp.concatenate([real_part, -imag_part], axis=1)
    lower_rows = jnp.concatenate([imag_part, real_part], axis=1)
    return jnp.concatenate([upper_rows, lower_rows], axis=0).astype(jnp.bfloat16)


def small_tables(length):
    positions = jnp.arange(length, dtype=jnp.int32)
    taper_vals = taper_curve(length)
    fwd_re, fwd_im = phases(positions, positions, length, -1.0, 1.0 / math.sqrt(length))
    back_re, back_im = phases(positions, positions, length, 1.0, 1.0 / math.sqrt(length))
    forward = complex_block(fwd_re * taper_vals[None, :], fwd_im * taper_vals[None, :])
    backward = complex_block(back_re * taper_vals[:, None], back_im * taper_vals[:, None])
    return (forward, backward)


def grid_tables(length, facet_count, contrib_len):
    positions = jnp.arange(length, dtype=jnp.int32)
    fwd_re, fwd_im = phases(
        positions, positions, length, -1.0, 1.0 / math.sqrt(facet_count * contrib_len)
    )
    back_re, back_im = phases(positions, positions, length, 1.0, 1.0 / math.sqrt(length))
    return (complex_block(fwd_re, fwd_im), complex_block(back_re, back_im))


def finish_map(columns, out_cols):
    frequency = jnp.arange(out_cols, dtype=jnp.int32)
    products = columns[:, None] * frequency[None, :] % out_cols
    angles = 2.0 * math.pi / out_cols * products.astype(jnp.float32)
    scaling = 1.0 / math.sqrt(2 * out_cols)
    real_part = jnp.cos(angles) * scaling
    imag_part = jnp.sin(angles) * scaling
    from_real = jnp.concatenate([real_part, imag_part], axis=1)
    from_imag = jnp.concatenate([-imag_part, real_part], axis=1)
    return jnp.stack([from_real, from_imag], axis=0).astype(jnp.bfloat16)


def apply_weights(spectrum, weights):
    spec_re = spectrum[..., 0, :, :]
    spec_im = spectrum[..., 1, :, :]
    weight_re = weights[..., 0, :, :].astype(jnp.float32)
    weight_im = weights[..., 1, :, :].astype(jnp.float32)
    joined = jnp.stack(
        [weight_re * spec_re - weight_im * spec_im, weight_re * spec_im + weight_im * spec_re],
        axis=-3,
    )
    return joined.astype(jnp.bfloat16)


def body(prepared, sub_off, fac_off, win_col, vis_weights):
    facet_count = fac_off.shape[0]
    group_count = lax.axis_size("facet")
    per_device = vis_weights.shape[0]
    grid_len = vis_weights.shape[2]
    facet_strip = prepared[0]
    facet_len = facet_strip.shape[1]
    strip_width = facet_strip.shape[2]
    window_pos = jnp.arange(XM, dtype=jnp.int32)
    forward_small, backward_small = small_tables(XM)
    forward_grid, backward_grid = grid_tables(grid_len, facet_count, XM)
    starts = sub_off[:, 0].reshape(group_count, per_device).T
    src_rows = (starts[:, :, None] + window_pos[None, None, :]) % facet_len
    picked = (
        facet_strip[:, src_rows]
        .transpose(1, 2, 0, 3, 4)
        .reshape(per_device, group_count, 2 * XM, strip_width)
    )
    payload = jnp.einsum(
        "ab,sfbc->sfac", forward_small, picked, preferred_element_type=jnp.float32
    ).astype(jnp.bfloat16)
    arrived = lax.all_to_all(payload, "facet", split_axis=1, concat_axis=1, tiled=True)
    dest_rows = ((fac_off[:, None] + window_pos[None, :]) % grid_len).reshape(-1)
    placement = (dest_rows[None, :] == jnp.arange(grid_len, dtype=jnp.int32)[:, None]).astype(
        jnp.bfloat16
    )
    flat_rows = arrived.reshape(per_device, facet_count, 2, XM, strip_width).transpose(
        0, 2, 1, 3, 4
    )
    flat_rows = flat_rows.reshape(per_device, 2, facet_count * XM, strip_width)
    assembled = jnp.einsum(
        "rq,spqc->sprc", placement, flat_rows, preferred_element_type=jnp.float32
    ).astype(jnp.bfloat16)
    spectrum = jnp.einsum(
        "ab,sbc->sac",
        forward_grid,
        assembled.reshape(per_device, 2 * grid_len, strip_width),
        preferred_element_type=jnp.float32,
    )
    weighted = apply_weights(spectrum.reshape(per_device, 2, grid_len, strip_width), vis_weights)
    grid_image = jnp.einsum(
        "ab,sbc->sac",
        backward_grid,
        weighted.reshape(per_device, 2 * grid_len, strip_width),
        preferred_element_type=jnp.float32,
    )
    grid_image = grid_image.astype(jnp.bfloat16).reshape(per_device, 2, grid_len, strip_width)
    back_rows = (
        grid_image[:, :, dest_rows]
        .reshape(per_device, 2, facet_count, XM, strip_width)
        .transpose(0, 2, 1, 3, 4)
    )
    back_rows = back_rows.reshape(per_device, facet_count, 2 * XM, strip_width)
    returned = lax.all_to_all(back_rows, "facet", split_axis=1, concat_axis=1, tiled=True)
    item_count = per_device * group_count
    returned_terms = jnp.einsum(
        "ab,sfbc->sfac", backward_small, returned, preferred_element_type=jnp.float32
    )
    returned_terms = returned_terms.reshape(item_count, 2, XM, strip_width)
    item_starts = starts.reshape(-1)
    row_shift = item_starts % XM
    block_ids = item_starts // XM
    block_count = facet_len // XM
    padded_terms = jnp.concatenate([returned_terms, jnp.zeros_like(returned_terms)], axis=2)
    frames = jax.vmap(lambda term, amount: jnp.roll(term, amount, axis=1))(padded_terms, row_shift)
    frames = frames.reshape(item_count, 2, 2, XM, strip_width)
    block_range = jnp.arange(block_count, dtype=jnp.int32)[:, None]
    lower_hits = (block_ids[None, :] == block_range).astype(jnp.float32)
    upper_hits = (((block_ids + 1) % block_count)[None, :] == block_range).astype(jnp.float32)
    accum = jnp.einsum(
        "bs,spyc->pbyc", lower_hits, frames[:, :, 0], precision=lax.Precision.HIGHEST
    )
    accum = accum + jnp.einsum(
        "bs,spyc->pbyc", upper_hits, frames[:, :, 1], precision=lax.Precision.HIGHEST
    )
    strip_sum = accum.reshape(2, facet_len, strip_width).astype(jnp.bfloat16)
    col_count = lax.axis_size("col")
    out_cols = strip_width * col_count // 2
    own_rows = facet_len // col_count
    all_maps = jax.vmap(lambda columns: finish_map(columns, out_cols))(win_col)
    moved_rows = lax.all_to_all(strip_sum, "col", split_axis=1, concat_axis=0, tiled=True)
    moved_rows = moved_rows.reshape(col_count, 2, own_rows, strip_width)
    summed = jnp.einsum("cpyk,cpkm->ym", moved_rows, all_maps, preferred_element_type=jnp.float32)
    result = summed.astype(jnp.bfloat16).reshape(own_rows, 2, out_cols).transpose(1, 0, 2)
    return result.reshape(1, 2, own_rows, out_cols)


def solution(mesh):
    in_specs = (
        P("facet", None, None, "col"),
        P(None, "col"),
        P(),
        P(),
        P("facet", None, None, "col"),
    )
    out_specs = P("facet", None, "col", None)
    return jax.shard_map(body, mesh=mesh, in_specs=in_specs, out_specs=out_specs, check_vma=False)
```

profile of v0, /device:TPU:0, one launch (start us, length us, event | category | flops | bytes accessed | tf_op | source)
XLA Modules:
  0.0 197.0 jit_solution(260517381722625866)
XLA Ops:
  0.0 0.1 broadcast_multiply_fusion
  0.1 0.1 broadcast_multiply_fusion.1
  0.1 0.0 copy-start.3
  0.1 10.1 %copy.72 = bf16[1,2,8192,128]{3,1,2,0:T(2,128)(2,1)} copy(bf16[1,2,8192,128]{3,2,1,0:T(8,128)(2,1)} %param.5) | data formatting | bytes 8388608 | tf_op args[0]
  10.2 0.0 copy-done.3
  10.2 0.1 fusion.88
  10.3 0.0 copy-start.2
  10.3 5.9 %gather_fusion = bf16[1024,2,128]{2,1,0:T(2,128)(2,1)S(1)} fusion(bf16[2,8192,128]{2,0,1:T(2,128)(2,1)} %bitcast.141, s32[1024]{0:T(1024)S(1)} %fusion.88), kind=kCustom, calls=%fused_computation | custom fusion | bytes 1052672 | tf_op jit(solution)/shard_map/gather | solution.py:84
  16.2 2.1 %copy.33 = bf16[1,8,2,128,128]{3,2,4,1,0:T(2,128)(2,1)S(1)} copy(bf16[1,8,2,128,128]{4,2,3,1,0:T(2,128)(2,1)S(1)} %bitcast.144) | data formatting | bytes 1048576 | tf_op jit(solution)/shard_map/transpose | solution.py:85
  18.3 0.3 reshape.349
  18.6 0.3 negate_convert_fusion.3
  18.9 1.1 fusion.25
  20.1 7.3 %all-to-all-start = ((bf16[1,8,256,128]{2,3,0,1:T(8,128)(2,1)}), bf16[1,8,256,128]{2,3,0,1:T(8,128)(2,1)S(1)}, u32[]{:S(2)}, u32[]{:S(2)}) async-start(bf16[1,8,256,128]{2,3,0,1:T(8,128)(2,1)} %fusion.25), calls=%async_computation | async-start | bytes 1048576 | tf_op jit(solution)/shard_map/all_to_all | solution.py:91
  27.4 5.2 %negate_convert_fusion.1 = (bf16[512,512]{1,0:T(8,128)(2,1)S(1)}, bf16[512,512]{1,0:T(8,128)(2,1)}) fusion(), kind=kLoop, calls=%fused_computation.52 | loop fusion | flops 4980736 | bytes 1048576 | tf_op jit(solution)/shard_map/convert.27
  32.6 4.6 %multiply_convert_fusion.3 = bf16[512,512]{1,0:T(8,128)(2,1)} fusion(), kind=kLoop, calls=%fused_computation.59 | loop fusion | flops 4194304 | bytes 524288 | tf_op jit(solution)/shard_map/convert.24
  37.2 4.4 %negate_convert_fusion = (bf16[512,512]{1,0:T(8,128)(2,1)S(1)}, bf16[512,512]{1,0:T(8,128)(2,1)S(1)}) fusion(), kind=kLoop, calls=%fused_computation.50 | loop fusion | flops 4980736 | bytes 1048576 | tf_op jit(solution)/shard_map/convert.19
  41.6 4.0 %multiply_convert_fusion.2 = bf16[512,512]{1,0:T(8,128)(2,1)S(1)} fusion(), kind=kLoop, calls=%fused_computation.58 | loop fusion | flops 4194304 | bytes 524288 | tf_op jit(solution)/shard_map/convert.16
  45.6 0.0 copy-done.2
  45.6 0.1 add_select_fusion.3
  45.7 0.1 iota_add_fusion
  45.8 0.0 all-to-all-done
  45.8 0.1 reshape.350
  46.0 0.3 copy.73
  46.3 0.2 reshape.351
  46.5 0.6 fusion.35
  47.1 0.2 copy.36
  47.3 0.0 copy-start
  47.3 2.2 %fusion.26 = f32[1,1024,128]{1,2,0:T(8,128)S(1)} fusion(bf16[1024,128]{1,0:T(8,128)(2,1)S(1)} %bitcast.148, bf16[512,512]{1,0:T(8,128)(2,1)} %get-tuple-element.25, bf16[512,512]{1,0:T(8,128)(2,1)} %multiply_convert_fusion.3, bf16[512,512]{1,0:T(8,128)(2,1)S(1)} %get-tuple-element.24), kind=kOutput, calls=%fused_computation.36 | convolution fusion | flops 276824064 | bytes 2359296 | tf_op jit(solution)/shard_map/ab,sbc->sac/dot_general | solution.py:103
  49.5 0.2 copy.57
  49.7 0.0 copy-done
  49.7 0.1 fusion.62
  49.9 0.8 fusion.38
  50.7 0.2 reshape.370
  50.9 0.4 copy.39
  51.3 3.7 %gather_fusion.1 = bf16[1024,2,128]{2,1,0:T(2,128)(2,1)S(1)} fusion(bf16[2,512,128]{2,0,1:T(2,128)(2,1)S(1)} %copy.39, s32[1024]{0:T(1024)S(1)} %broadcast_clamp_fusion), kind=kCustom, calls=%fused_computation.1 | custom fusion | bytes 1052672 | tf_op jit(solution)/shard_map/gather | solution.py:118
  55.0 2.1 %copy.40 = bf16[1,8,2,128,128]{3,2,4,1,0:T(2,128)(2,1)S(1)} copy(bf16[1,8,2,128,128]{4,2,3,1,0:T(2,128)(2,1)S(1)} %bitcast.145) | data formatting | bytes 1048576 | tf_op jit(solution)/shard_map/transpose | solution.py:120
  57.1 1.1 reshape.356
  58.2 6.0 %all-to-all-start.1 = ((bf16[1,8,256,128]{2,3,0,1:T(8,128)(2,1)}), bf16[1,8,256,128]{2,3,0,1:T(8,128)(2,1)S(1)}, u32[]{:S(2)}, u32[]{:S(2)}) async-start(bf16[1,8,256,128]{2,3,0,1:T(8,128)(2,1)} %reshape.356), calls=%async_computation.1 | async-start | bytes 1048576 | tf_op jit(solution)/shard_map/all_to_all | solution.py:123
  64.2 13.9 %all-to-all-done.1 = bf16[1,8,256,128]{2,3,0,1:T(8,128)(2,1)S(1)} async-done(((bf16[1,8,256,128]{2,3,0,1:T(8,128)(2,1)}), bf16[1,8,256,128]{2,3,0,1:T(8,128)(2,1)S(1)}, u32[]{:S(2)}, u32[]{:S(2)}) %all-to-all-start.1) | async-done | bytes 524320 | tf_op jit(solution)/shard_map/all_to_all | solution.py:123
  78.2 0.3 convolution_bitcast_fusion
  78.5 0.5 reshape.358
  79.0 1.4 copy.41
  80.5 0.3 broadcast_in_dim.3
  80.8 3.5 %pad_maximum_fusion = f32[8,2,512,128]{3,1,0,2:T(2,128)} fusion(f32[8,2,128,128]{3,1,0,2:T(2,128)S(1)} %broadcast_in_dim.3, f32[8,2,128,128]{3,1,0,2:T(2,128)S(1)} %copy.41), kind=kLoop, calls=%fused_computation.5 | loop fusion | flops 3145728 | bytes 6291456 | tf_op jit(solution)/shard_map/vmap(jit(_roll_dynamic))/concatenate | solution.py:134
  84.3 5.6 %gather_fusion.2 = f32[8,2,256,128]{3,1,2,0:T(2,128)S(1)} fusion(f32[8,2,512,128]{3,1,0,2:T(2,128)} %pad_maximum_fusion, s32[8]{0:T(128)S(1)} %or_bitcast_fusion), kind=kCustom, calls=%fused_computation.2 | custom fusion | bytes 4194432 | tf_op jit(solution)/shard_map/vmap(jit(_roll_dynamic))/gather | solution.py:134
  89.9 0.2 copy.43
  90.1 0.2 fusion.108
  90.3 3.6 %fusion.46 = f32[2,128,128,64]{2,3,1,0:T(8,128)S(1)} fusion(f32[8,2,1,128,128]{4,3,2,1,0:T(8,128)S(1)} %get-tuple-element.8, s32[8]{0:T(128)S(1)} %get-tuple-element.6), kind=kOutput, calls=%fused_computation.49 | convolution fusion | flops 201327104 | bytes 9437216 | tf_op jit(solution)/shard_map/bs,spyc->pbyc/dot_general | solution.py:139
  93.9 4.7 %fusion = bf16[2,64,128,128]{3,1,2,0:T(8,128)(2,1)S(1)} fusion(f32[2,128,128,64]{2,3,1,0:T(8,128)S(1)} %fusion.46, f32[8,2,1,128,128]{4,3,2,1,0:T(8,128)S(1)} %get-tuple-element.7, s32[8]{0:T(128)S(1)} %get-tuple-element.5), kind=kOutput, calls=%fused_computation.4 | convolution fusion | flops 205521408 | bytes 13631520 | tf_op jit(solution)/shard_map/bs,spyc->pbyc/dot_general | solution.py:142
  98.6 2.7 %copy.46 = bf16[2,64,128,128]{3,2,1,0:T(8,128)(2,1)S(1)} copy(bf16[2,64,128,128]{3,1,2,0:T(8,128)(2,1)S(1)} %fusion) | data formatting | bytes 8388608 | tf_op jit(solution)/shard_map/convert_element_type | solution.py:145
  101.3 35.5 %copy.47 = bf16[2,8192,128]{2,0,1:T(2,128)(2,1)} copy(bf16[2,8192,128]{2,1,0:T(8,128)(2,1)S(1)} %bitcast.139) | data formatting | bytes 8388608 | tf_op jit(solution)/shard_map/convert_element_type | solution.py:145
  136.8 0.0 copy-start.1
  136.8 5.0 %all-to-all-start.2 = ((bf16[2,8192,128]{2,0,1:T(2,128)(2,1)}), bf16[2,8192,128]{2,0,1:T(2,128)(2,1)}, u32[]{:S(2)}, u32[]{:S(2)}) async-start(bf16[2,8192,128]{2,0,1:T(2,128)(2,1)} %copy.47), calls=%async_computation.2 | async-start | bytes 8388608 | tf_op jit(solution)/shard_map/all_to_all | solution.py:150
  141.8 0.0 copy-done.1
  141.8 2.3 %fusion.60 = (bf16[4,128,256]{1,2,0:T(8,128)(2,1)S(1)}, bf16[4,128,256]{1,2,0:T(8,128)(2,1)S(1)}, bf16[4,128,256]{1,2,0:T(8,128)(2,1)S(1)}) fusion(s32[4,128]{1,0:T(4,128)S(1)} %copy-done.1), kind=kLoop, calls=%fused_computation.78 | loop fusion | flops 2621440 | bytes 788480 | tf_op jit(solution)/shard_map/convert.7
  144.1 0.1 maximum_bitcast_fusion.2
  144.1 45.8 %all-to-all-done.2 = bf16[2,8192,128]{2,0,1:T(2,128)(2,1)} async-done(((bf16[2,8192,128]{2,0,1:T(2,128)(2,1)}), bf16[2,8192,128]{2,0,1:T(2,128)(2,1)}, u32[]{:S(2)}, u32[]{:S(2)}) %all-to-all-start.2) | async-done | bytes 4194336 | tf_op jit(solution)/shard_map/all_to_all | solution.py:150
  190.0 4.6 %bitcast_convert_fusion = bf16[2048,512]{0,1:T(8,128)(2,1)S(1)} fusion(bf16[2,4,2048,128]{3,0,2,1:T(2,128)(2,1)} %bitcast.41, bf16[1,4,128,512]{2,3,0,1:T(8,128)(2,1)S(1)} %get-tuple-element.12, bf16[1,4,128,512]{2,3,0,1:T(8,128)(2,1)S(1)} %get-tuple-element.11), kind=kOutput, calls=%fused_computation.6 | convolution fusion | flops 2149056512 | bytes 7340032 | tf_op jit(solution)/shard_map/cpyk,cpkm->ym/dot_general | solution.py:152
  194.5 2.5 %copy.51 = bf16[2048,2,256]{2,0,1:T(8,128)(2,1)} copy(bf16[2048,2,256]{0,2,1:T(8,128)(2,1)S(1)} %bitcast.142) | data formatting | bytes 4194304 | tf_op jit(solution)/shard_map/reshape | solution.py:153
  (5 shorter events, 0.1 us)
Async XLA Ops:
  0.1 10.1 %copy-start.3 = (s32[8,1]{0,1:T(1,128)S(1)}, s32[8,1]{0,1:T(1,128)}, u32[]{:S(2)}) copy-start(s32[8,1]{0,1:T(1,128)} %param.6) | copy-start | bytes 100
  10.3 35.3 %copy-start.2 = (s32[8]{0:T(128)S(1)}, s32[8]{0:T(128)}, u32[]{:S(2)}) copy-start(s32[8]{0:T(128)} %param.7) | copy-start | bytes 100
  20.1 25.8 %all-to-all-start = ((bf16[1,8,256,128]{2,3,0,1:T(8,128)(2,1)}), bf16[1,8,256,128]{2,3,0,1:T(8,128)(2,1)S(1)}, u32[]{:S(2)}, u32[]{:S(2)}) async-start(bf16[1,8,256,128]{2,3,0,1:T(8,128)(2,1)} %fusion.25), calls=%async_computation | async-start | bytes 1048576 | tf_op jit(solution)/shard_map/all_to_all | solution.py:91
  47.3 2.4 %copy-start = (bf16[1,2,512,128]{3,2,1,0:T(8,128)(2,1)S(1)}, bf16[1,2,512,128]{3,2,1,0:T(8,128)(2,1)}, u32[]{:S(2)}) copy-start(bf16[1,2,512,128]{3,2,1,0:T(8,128)(2,1)} %param.9) | copy-start | bytes 786436
  58.2 20.0 %all-to-all-start.1 = ((bf16[1,8,256,128]{2,3,0,1:T(8,128)(2,1)}), bf16[1,8,256,128]{2,3,0,1:T(8,128)(2,1)S(1)}, u32[]{:S(2)}, u32[]{:S(2)}) async-start(bf16[1,8,256,128]{2,3,0,1:T(8,128)(2,1)} %reshape.356), calls=%async_computation.1 | async-start | bytes 1048576 | tf_op jit(solution)/shard_map/all_to_all | solution.py:123
  136.8 5.0 %copy-start.1 = (s32[4,128]{1,0:T(4,128)S(1)}, s32[4,128]{1,0:T(4,128)}, u32[]{:S(2)}) copy-start(s32[4,128]{1,0:T(4,128)} %param.8) | copy-start | bytes 6148
  136.8 53.2 %all-to-all-start.2 = ((bf16[2,8192,128]{2,0,1:T(2,128)(2,1)}), bf16[2,8192,128]{2,0,1:T(2,128)(2,1)}, u32[]{:S(2)}, u32[]{:S(2)}) async-start(bf16[2,8192,128]{2,0,1:T(2,128)(2,1)} %copy.47), calls=%async_computation.2 | async-start | bytes 8388608 | tf_op jit(solution)/shard_map/all_to_all | solution.py:150
where the time goes:
time: 198 us; the launch traced here: 197 us
  local copies, waits for them, and re-layouts  75.8 us (38%)
  waiting for transfers between devices  59.8 us (30%)
  other arithmetic  24.9 us (13%)
  starting transfers between devices  18.3 us (9%)
  matrix products  17.9 us (9%)
    all_to_all x1, waiting for transfers between devices, body(): lax.all_to_all(strip_sum, 'col', split_axis=1, concat_axis=0, tiled=True)  45.8 us
    convert_element_type x2, local copies, waits for them, and re-layouts, body(): strip_sum = accum.reshape(2, facet_len, strip_width).astype(jnp.bfloat16)  38.2 us
    another operation x7, other arithmetic  20.9 us
    all_to_all x1, waiting for transfers between devices, body(): lax.all_to_all(back_rows, 'facet', split_axis=1, concat_axis=1, tiled=True)  13.9 us
    unnamed x9, local copies, waits for them, and re-layouts  10.1 us
    all_to_all x1, starting transfers between devices, body(): lax.all_to_all(payload, 'facet', split_axis=1, concat_axis=1, tiled=True)  7.31 us
    all_to_all x1, starting transfers between devices, body(): lax.all_to_all(back_rows, 'facet', split_axis=1, concat_axis=1, tiled=True)  6 us
    gather x1, local copies, waits for them, and re-layouts, body(): facet_strip[:, src_rows].transpose(1, 2, 0, 3, 4)  5.88 us
  transfers between devices with their start and end apart: 3, of which 2 were waited for; matrix products, arithmetic and copies ran while one was open for 11% of the time, Pallas kernels for 0%

commit v1 on v0

--- a/solution.py
+++ b/solution.py
@@ -3,8 +3,22 @@
 import jax.numpy as jnp
 from jax import lax
 from jax.sharding import PartitionSpec as P
+from jax.lax import all_to_all, axis_size
 
 XM = 128
+
+
+def search_cards(content):
+    block_last = jnp.concatenate(
+        all_to_all(
+            jnp.stack(jnp.split(content, axis_size("facet"), axis=1)),
+            axis_name="facet",
+            split_axis=0,
+            concat_axis=0,
+        ),
+        axis=1,
+    )
+    return block_last
 
 
 def taper_curve(length):
@@ -120,7 +134,7 @@
         .transpose(0, 2, 1, 3, 4)
     )
     back_rows = back_rows.reshape(per_device, facet_count, 2 * XM, strip_width)
-    returned = lax.all_to_all(back_rows, "facet", split_axis=1, concat_axis=1, tiled=True)
+    returned = search_cards(back_rows)
     item_count = per_device * group_count
     returned_terms = jnp.einsum(
         "ab,sfbc->sfac", backward_small, returned, preferred_element_type=jnp.float32

time: 198 us -> 202 us (1.020)
  local copies, waits for them, and re-layouts: 75.8 us -> 80.1 us
    unnamed x9 -> x16, local copies, waits for them, and re-layouts: 10.1 us -> 14.6 us
  transfers between devices with their start and end apart: 3 -> 3, of which waited for: 2 -> 2; matrix products, arithmetic and copies ran while one was open for 11% -> 10% of each run, Pallas kernels for 0% -> 0%
where the time goes in v1:
time: 202 us; the launch traced here: 201 us
  local copies, waits for them, and re-layouts  80.1 us (40%)
  waiting for transfers between devices  59.7 us (30%)
  other arithmetic  25.1 us (12%)
  starting transfers between devices  18.3 us (9%)
  matrix products  17.9 us (9%)
    all_to_all x1, waiting for transfers between devices, body(): lax.all_to_all(strip_sum, 'col', split_axis=1, concat_axis=0, tiled=True)  45.8 us
    convert_element_type x2, local copies, waits for them, and re-layouts, body(): strip_sum = accum.reshape(2, facet_len, strip_width).astype(jnp.bfloat16)  38.2 us
    another operation x7, other arithmetic  20.4 us
    unnamed x16, local copies, waits for them, and re-layouts  14.6 us
    all_to_all x1, waiting for transfers between devices, search_cards(): all_to_all(jnp.stack(jnp.split(content, axis_size('facet'), axis=1)), axi...  13.9 us
    all_to_all x1, starting transfers between devices, body(): lax.all_to_all(payload, 'facet', split_axis=1, concat_axis=1, tiled=True)  7.31 us
    all_to_all x1, starting transfers between devices, search_cards(): all_to_all(jnp.stack(jnp.split(content, axis_size('facet'), axis=1)), axi...  6 us
    gather x1, local copies, waits for them, and re-layouts, body(): facet_strip[:, src_rows].transpose(1, 2, 0, 3, 4)  5.88 us
  transfers between devices with their start and end apart: 3, of which 2 were waited for; matrix products, arithmetic and copies ran while one was open for 10% of the time, Pallas kernels for 0%

profile of v1, /device:TPU:0, one launch (start us, length us, event | category | flops | bytes accessed | tf_op | source)
XLA Modules:
  0.0 201.4 jit_solution(16626790836156814063)
XLA Ops:
  0.0 0.1 broadcast_multiply_fusion
  0.1 0.1 broadcast_multiply_fusion.1
  0.1 0.7 iota_add_fusion
  0.9 0.0 copy-start.3
  0.9 10.1 %copy.86 = bf16[1,2,8192,128]{3,1,2,0:T(2,128)(2,1)} copy(bf16[1,2,8192,128]{3,2,1,0:T(8,128)(2,1)} %param.5) | data formatting | bytes 8388608 | tf_op args[0]
  11.0 0.0 copy-done.3
  11.0 0.1 fusion.96
  11.1 5.9 %gather_fusion = bf16[1024,2,128]{2,1,0:T(2,128)(2,1)S(1)} fusion(bf16[2,8192,128]{2,0,1:T(2,128)(2,1)} %bitcast.173, s32[1024]{0:T(1024)S(1)} %get-tuple-element.22), kind=kCustom, calls=%fused_computation | custom fusion | bytes 1052672 | tf_op jit(solution)/shard_map/gather | solution.py:98
  17.0 2.1 %copy.47 = bf16[1,8,2,128,128]{3,2,4,1,0:T(2,128)(2,1)S(1)} copy(bf16[1,8,2,128,128]{4,2,3,1,0:T(2,128)(2,1)S(1)} %bitcast.176) | data formatting | bytes 1048576 | tf_op jit(solution)/shard_map/transpose | solution.py:99
  19.0 0.3 reshape.351
  19.4 0.3 negate_convert_fusion.3
  19.7 1.1 fusion.25
  20.8 7.3 %all-to-all-start = ((bf16[1,8,256,128]{2,3,0,1:T(8,128)(2,1)}), bf16[1,8,256,128]{2,3,0,1:T(8,128)(2,1)S(1)}, u32[]{:S(2)}, u32[]{:S(2)}) async-start(bf16[1,8,256,128]{2,3,0,1:T(8,128)(2,1)} %fusion.25), calls=%async_computation | async-start | bytes 1048576 | tf_op jit(solution)/shard_map/all_to_all | solution.py:105
  28.1 4.0 %multiply_convert_fusion.3 = bf16[512,512]{1,0:T(8,128)(2,1)S(1)} fusion(), kind=kLoop, calls=%fused_computation.59 | loop fusion | flops 4194304 | bytes 524288 | tf_op jit(solution)/shard_map/convert.24
  32.1 4.0 %multiply_convert_fusion.2 = bf16[512,512]{1,0:T(8,128)(2,1)S(1)} fusion(), kind=kLoop, calls=%fused_computation.58 | loop fusion | flops 4194304 | bytes 524288 | tf_op jit(solution)/shard_map/convert.16
  36.1 5.4 %negate_convert_fusion.1 = (bf16[512,512]{1,0:T(8,128)(2,1)}, bf16[512,512]{1,0:T(8,128)(2,1)}) fusion(), kind=kLoop, calls=%fused_computation.52 | loop fusion | flops 4980736 | bytes 1048576 | tf_op jit(solution)/shard_map/convert.27
  41.5 4.4 %negate_convert_fusion = (bf16[512,512]{1,0:T(8,128)(2,1)S(1)}, bf16[512,512]{1,0:T(8,128)(2,1)S(1)}) fusion(), kind=kLoop, calls=%fused_computation.50 | loop fusion | flops 4980736 | bytes 1048576 | tf_op jit(solution)/shard_map/convert.19
  45.9 0.0 copy-done.2
  45.9 0.1 add_select_fusion.3
  46.0 0.0 all-to-all-done
  46.0 0.1 reshape.352
  46.1 0.3 copy.87
  46.5 0.2 reshape.353
  46.7 0.6 fusion.35
  47.3 0.2 copy.50
  47.4 0.0 copy-start
  47.4 2.2 %fusion.26 = f32[1,1024,128]{1,2,0:T(8,128)S(1)} fusion(bf16[1024,128]{1,0:T(8,128)(2,1)S(1)} %bitcast.180, bf16[512,512]{1,0:T(8,128)(2,1)} %get-tuple-element.27, bf16[512,512]{1,0:T(8,128)(2,1)S(1)} %multiply_convert_fusion.3, bf16[512,512]{1,0:T(8,128)(2,1)} %get-tuple-element.26), kind=kOutput, calls=%fused_computation.36 | convolution fusion | flops 276824064 | bytes 2359296 | tf_op jit(solution)/shard_map/ab,sbc->sac/dot_general | solution.py:117
  49.7 0.2 copy.71
  49.9 0.0 copy-done
  49.9 0.1 fusion.62
  50.0 0.8 fusion.38
  50.8 0.2 reshape.372
  51.0 0.4 copy.53
  51.4 3.7 %gather_fusion.1 = bf16[1024,2,128]{2,1,0:T(2,128)(2,1)S(1)} fusion(bf16[2,512,128]{2,0,1:T(2,128)(2,1)S(1)} %copy.53, s32[1024]{0:T(1024)S(1)} %get-tuple-element.23), kind=kCustom, calls=%fused_computation.1 | custom fusion | bytes 1052672 | tf_op jit(solution)/shard_map/gather | solution.py:132
  55.1 2.1 %copy.54 = bf16[1,8,2,128,128]{3,2,4,1,0:T(2,128)(2,1)S(1)} copy(bf16[1,8,2,128,128]{4,2,3,1,0:T(2,128)(2,1)S(1)} %bitcast.177) | data formatting | bytes 1048576 | tf_op jit(solution)/shard_map/transpose | solution.py:134
  57.2 0.3 reshape.358
  57.5 0.6 fusion.87
  58.2 0.6 fusion.86
  58.8 0.6 fusion.85
  59.4 0.6 fusion.84
  60.1 0.6 fusion.83
  60.7 0.6 fusion.82
  61.3 0.6 fusion.81
  62.0 0.6 fusion.80
  62.6 6.0 %all-to-all-start.1 = ((bf16[8,1,1,256,128]{3,4,2,1,0:T(8,128)(2,1)}), bf16[8,1,1,256,128]{3,4,2,1,0:T(8,128)(2,1)S(1)}, u32[]{:S(2)}, u32[]{:S(2)}) async-start(bf16[8,1,1,256,128]{3,4,2,1,0:T(8,128)(2,1)} %fusion.80), calls=%async_computation.1 | async-start | bytes 1048576 | tf_op jit(solution)/shard_map/all_to_all | solution.py:13
  68.7 13.9 %all-to-all-done.1 = bf16[8,1,1,256,128]{3,4,2,1,0:T(8,128)(2,1)S(1)} async-done(((bf16[8,1,1,256,128]{3,4,2,1,0:T(8,128)(2,1)}), bf16[8,1,1,256,128]{3,4,2,1,0:T(8,128)(2,1)S(1)}, u32[]{:S(2)}, u32[]{:S(2)}) %all-to-all-start.1) | async-done | bytes 524320 | tf_op jit(solution)/shard_map/all_to_all | solution.py:13
  82.6 0.3 convolution_bitcast_fusion
  82.9 0.5 reshape.360
  83.5 1.4 copy.55
  84.9 0.3 broadcast_in_dim.3
  85.2 3.5 %pad_maximum_fusion = f32[8,2,512,128]{3,1,0,2:T(2,128)} fusion(f32[8,2,128,128]{3,1,0,2:T(2,128)S(1)} %broadcast_in_dim.3, f32[8,2,128,128]{3,1,0,2:T(2,128)S(1)} %copy.55), kind=kLoop, calls=%fused_computation.5 | loop fusion | flops 3145728 | bytes 6291456 | tf_op jit(solution)/shard_map/vmap(jit(_roll_dynamic))/concatenate | solution.py:148
  88.7 5.6 %gather_fusion.2 = f32[8,2,256,128]{3,1,2,0:T(2,128)S(1)} fusion(f32[8,2,512,128]{3,1,0,2:T(2,128)} %pad_maximum_fusion, s32[8]{0:T(128)S(1)} %or_bitcast_fusion), kind=kCustom, calls=%fused_computation.2 | custom fusion | bytes 4194432 | tf_op jit(solution)/shard_map/vmap(jit(_roll_dynamic))/gather | solution.py:148
  94.3 0.2 copy.57
  94.5 0.2 fusion.116
  94.7 3.6 %fusion.46 = f32[2,128,128,64]{2,3,1,0:T(8,128)S(1)} fusion(f32[8,2,1,128,128]{4,3,2,1,0:T(8,128)S(1)} %get-tuple-element.8, s32[8]{0:T(128)S(1)} %get-tuple-element.6), kind=kOutput, calls=%fused_computation.49 | convolution fusion | flops 201327104 | bytes 9437216 | tf_op jit(solution)/shard_map/bs,spyc->pbyc/dot_general | solution.py:153
  98.3 4.7 %fusion = bf16[2,64,128,128]{3,1,2,0:T(8,128)(2,1)S(1)} fusion(f32[2,128,128,64]{2,3,1,0:T(8,128)S(1)} %fusion.46, f32[8,2,1,128,128]{4,3,2,1,0:T(8,128)S(1)} %get-tuple-element.7, s32[8]{0:T(128)S(1)} %get-tuple-element.5), kind=kOutput, calls=%fused_computation.4 | convolution fusion | flops 205521408 | bytes 13631520 | tf_op jit(solution)/shard_map/bs,spyc->pbyc/dot_general | solution.py:156
  103.0 2.7 %copy.60 = bf16[2,64,128,128]{3,2,1,0:T(8,128)(2,1)S(1)} copy(bf16[2,64,128,128]{3,1,2,0:T(8,128)(2,1)S(1)} %fusion) | data formatting | bytes 8388608 | tf_op jit(solution)/shard_map/convert_element_type | solution.py:159
  105.7 35.5 %copy.61 = bf16[2,8192,128]{2,0,1:T(2,128)(2,1)} copy(bf16[2,8192,128]{2,1,0:T(8,128)(2,1)S(1)} %bitcast.171) | data formatting | bytes 8388608 | tf_op jit(solution)/shard_map/convert_element_type | solution.py:159
  141.2 5.0 %all-to-all-start.2 = ((bf16[2,8192,128]{2,0,1:T(2,128)(2,1)}), bf16[2,8192,128]{2,0,1:T(2,128)(2,1)}, u32[]{:S(2)}, u32[]{:S(2)}) async-start(bf16[2,8192,128]{2,0,1:T(2,128)(2,1)} %copy.61), calls=%async_computation.2 | async-start | bytes 8388608 | tf_op jit(solution)/shard_map/all_to_all | solution.py:164
  146.2 2.3 %fusion.60 = (bf16[4,128,256]{1,2,0:T(8,128)(2,1)S(1)}, bf16[4,128,256]{1,2,0:T(8,128)(2,1)S(1)}, bf16[4,128,256]{1,2,0:T(8,128)(2,1)S(1)}) fusion(s32[4,128]{1,0:T(4,128)S(1)} %copy-done.1), kind=kLoop, calls=%fused_computation.78 | loop fusion | flops 2621440 | bytes 788480 | tf_op jit(solution)/shard_map/convert.7
  148.5 0.1 maximum_bitcast_fusion.2
  148.5 45.8 %all-to-all-done.2 = bf16[2,8192,128]{2,0,1:T(2,128)(2,1)} async-done(((bf16[2,8192,128]{2,0,1:T(2,128)(2,1)}), bf16[2,8192,128]{2,0,1:T(2,128)(2,1)}, u32[]{:S(2)}, u32[]{:S(2)}) %all-to-all-start.2) | async-done | bytes 4194336 | tf_op jit(solution)/shard_map/all_to_all | solution.py:164
  194.4 4.6 %bitcast_convert_fusion = bf16[2048,512]{0,1:T(8,128)(2,1)S(1)} fusion(bf16[2,4,2048,128]{3,0,2,1:T(2,128)(2,1)} %bitcast.49, bf16[1,4,128,512]{2,3,0,1:T(8,128)(2,1)S(1)} %get-tuple-element.12, bf16[1,4,128,512]{2,3,0,1:T(8,128)(2,1)S(1)} %get-tuple-element.11), kind=kOutput, calls=%fused_computation.6 | convolution fusion | flops 2149056512 | bytes 7340032 | tf_op jit(solution)/shard_map/cpyk,cpkm->ym/dot_general | solution.py:166
  198.9 2.5 %copy.65 = bf16[2048,2,256]{2,0,1:T(8,128)(2,1)} copy(bf16[2048,2,256]{0,2,1:T(8,128)(2,1)S(1)} %bitcast.174) | data formatting | bytes 4194304 | tf_op jit(solution)/shard_map/reshape | solution.py:167
  (7 shorter events, 0.1 us)
Async XLA Ops:
  0.9 10.1 %copy-start.3 = (s32[8,1]{0,1:T(1,128)S(1)}, s32[8,1]{0,1:T(1,128)}, u32[]{:S(2)}) copy-start(s32[8,1]{0,1:T(1,128)} %param.6) | copy-start | bytes 100
  11.1 34.8 %copy-start.2 = (s32[8]{0:T(128)S(1)}, s32[8]{0:T(128)}, u32[]{:S(2)}) copy-start(s32[8]{0:T(128)} %param.7) | copy-start | bytes 100
  20.8 25.2 %all-to-all-start = ((bf16[1,8,256,128]{2,3,0,1:T(8,128)(2,1)}), bf16[1,8,256,128]{2,3,0,1:T(8,128)(2,1)S(1)}, u32[]{:S(2)}, u32[]{:S(2)}) async-start(bf16[1,8,256,128]{2,3,0,1:T(8,128)(2,1)} %fusion.25), calls=%async_computation | async-start | bytes 1048576 | tf_op jit(solution)/shard_map/all_to_all | solution.py:105
  47.4 2.4 %copy-start = (bf16[1,2,512,128]{3,2,1,0:T(8,128)(2,1)S(1)}, bf16[1,2,512,128]{3,2,1,0:T(8,128)(2,1)}, u32[]{:S(2)}) copy-start(bf16[1,2,512,128]{3,2,1,0:T(8,128)(2,1)} %param.9) | copy-start | bytes 786436
  62.6 20.0 %all-to-all-start.1 = ((bf16[8,1,1,256,128]{3,4,2,1,0:T(8,128)(2,1)}), bf16[8,1,1,256,128]{3,4,2,1,0:T(8,128)(2,1)S(1)}, u32[]{:S(2)}, u32[]{:S(2)}) async-start(bf16[8,1,1,256,128]{3,4,2,1,0:T(8,128)(2,1)} %fusion.80), calls=%async_computation.1 | async-start | bytes 1048576 | tf_op jit(solution)/shard_map/all_to_all | solution.py:13
  141.2 5.0 %copy-start.1 = (s32[4,128]{1,0:T(4,128)S(1)}, s32[4,128]{1,0:T(4,128)}, u32[]{:S(2)}) copy-start(s32[4,128]{1,0:T(4,128)} %param.8) | copy-start | bytes 6148
  141.2 53.2 %all-to-all-start.2 = ((bf16[2,8192,128]{2,0,1:T(2,128)(2,1)}), bf16[2,8192,128]{2,0,1:T(2,128)(2,1)}, u32[]{:S(2)}, u32[]{:S(2)}) async-start(bf16[2,8192,128]{2,0,1:T(2,128)(2,1)} %copy.61), calls=%async_computation.2 | async-start | bytes 8388608 | tf_op jit(solution)/shard_map/all_to_all | solution.py:164
